TPU v7x, 32 devices: a whole 2x2x4 slice. The times are simulated.
32 devices in a mesh: seq: 8 (over y, x, core), chan: 4 (over z).
Axes of the slice: x: 2, y: 2, z: 4, core: 2. Of those that a mesh axis runs over, the one named last changes fastest.
Arguments:
- queries: bfloat16 [8192, 4096], P('seq', 'chan'), may hold values from -6 to 6
- key_input: bfloat16 [8192, 4096], P('seq', 'chan'), may hold values from -6 to 6
- value_input: bfloat16 [8192, 4096], P('seq', 'chan'), may hold values from -6 to 6
- basis_filters: bfloat16 [8192, 256], P('seq'), may hold values from -0.0625 to 0.0625
- tucker_factor: bfloat16 [4096, 256], P('chan'), may hold values from -0.375 to 0.375
- skip_bias: float32 [4096], P('chan'), may hold values from -4 to 4
- cotangent: bfloat16 [8192, 4096], P('seq', 'chan'), may hold values from -6 to 6
Outputs:
- hyena_out: bfloat16 [8192, 4096], P('seq', 'chan')
- grad_query: bfloat16 [8192, 4096], P('seq', 'chan')
- grad_key: bfloat16 [8192, 4096], P('seq', 'chan')
- grad_value: bfloat16 [8192, 4096], P('seq', 'chan')
- grad_factor: float32 [4096, 256], P('chan')
- grad_basis: float32 [8192, 256], P('seq')
All inputs are finite; a program needn't handle non-finite values.
Results may differ from a plain program's by a relative error of at most 0.017.
Values may be sent and summed in bfloat16 or wider, within the bound.
A program may use at most 320 MiB of HBM per device.

v0:
```python
import math

import jax
import jax.numpy as jnp
from jax import lax
from jax.sharding import PartitionSpec as P

ACCURATE = lax.Precision.HIGH


def as_sent(shard):
    return jax.tree.map(lambda a: a.astype(jnp.bfloat16) if a.dtype == jnp.float32 else a, shard)


def split_length(length):
    padded_size = 2 * length
    inner_size = 1
    for candidate in range(1, length + 1):
        if candidate * candidate > padded_size:
            break
        if length % candidate == 0:
            inner_size = candidate
    return (inner_size, padded_size // inner_size)


def phase_table(rows_count, cols_count, period):
    row_index = jnp.arange(rows_count, dtype=jnp.int32)[:, None]
    col_index = jnp.arange(cols_count, dtype=jnp.int32)[None, :]
    product = row_index * col_index % period
    angles = product.astype(jnp.float32) * (2.0 * math.pi / period)
    return (jnp.cos(angles), -jnp.sin(angles))


def make_tables(length):
    inner_size, outer_size = split_length(length)
    cosine_inner, sine_inner = phase_table(inner_size, inner_size, inner_size)
    cosine_outer, sine_outer = phase_table(outer_size, outer_size, outer_size)
    cosine_twist, sine_twist = phase_table(outer_size, inner_size, 2 * length)
    return (cosine_inner, sine_inner, cosine_outer, sine_outer, cosine_twist, sine_twist)


def table_product(table, blocks):
    high_part = table.astype(jnp.bfloat16)
    low_part = (table - high_part.astype(jnp.float32)).astype(jnp.bfloat16)
    return jnp.einsum(
        "kn,cna->cka", high_part, blocks, preferred_element_type=jnp.float32
    ) + jnp.einsum("kn,cna->cka", low_part, blocks, preferred_element_type=jnp.float32)


def forward_real(signal, tables):
    cosine_inner, sine_inner, cosine_outer, sine_outer, cosine_twist, sine_twist = tables
    inner_size = cosine_inner.shape[0]
    outer_half = cosine_outer.shape[0] // 2
    blocks = signal.reshape(signal.shape[0], outer_half, inner_size)
    section_real = table_product(cosine_outer[:, :outer_half], blocks)
    section_imag = table_product(sine_outer[:, :outer_half], blocks)
    twist_real = section_real * cosine_twist - section_imag * sine_twist
    twist_imag = section_real * sine_twist + section_imag * cosine_twist
    spectrum_real = jnp.einsum(
        "cka,ja->ckj", twist_real, cosine_inner, precision=ACCURATE
    ) - jnp.einsum("cka,ja->ckj", twist_imag, sine_inner, precision=ACCURATE)
    spectrum_imag = jnp.einsum(
        "cka,ja->ckj", twist_real, sine_inner, precision=ACCURATE
    ) + jnp.einsum("cka,ja->ckj", twist_imag, cosine_inner, precision=ACCURATE)
    return (spectrum_real, spectrum_imag)


def inverse_real(spectrum_real, spectrum_imag, tables):
    cosine_inner, sine_inner, cosine_outer, sine_outer, cosine_twist, sine_twist = tables
    inner_size = cosine_inner.shape[0]
    outer_half = cosine_outer.shape[0] // 2
    section_real = jnp.einsum(
        "ckj,aj->cka", spectrum_real, cosine_inner, precision=ACCURATE
    ) + jnp.einsum("ckj,aj->cka", spectrum_imag, sine_inner, precision=ACCURATE)
    section_imag = jnp.einsum(
        "ckj,aj->cka", spectrum_imag, cosine_inner, precision=ACCURATE
    ) - jnp.einsum("ckj,aj->cka", spectrum_real, sine_inner, precision=ACCURATE)
    twist_real = section_real * cosine_twist + section_imag * sine_twist
    twist_imag = section_imag * cosine_twist - section_real * sine_twist
    signal = jnp.einsum(
        "nk,cka->cna", cosine_outer[:outer_half], twist_real, precision=ACCURATE
    ) + jnp.einsum("nk,cka->cna", sine_outer[:outer_half], twist_imag, precision=ACCURATE)
    padded_size = cosine_outer.shape[0] * inner_size
    return (signal / padded_size).reshape(signal.shape[0], outer_half * inner_size)


def convolve(mixed_chan, gated_chan, filter_chan, tables):
    stacked = jnp.concatenate((mixed_chan, gated_chan, filter_chan), 0)
    spectrum_real, spectrum_imag = forward_real(stacked, tables)
    mixed_real, gated_real, filter_real = jnp.split(spectrum_real, 3, 0)
    mixed_imag, gated_imag, filter_imag = jnp.split(spectrum_imag, 3, 0)
    output_real = filter_real * mixed_real - filter_imag * mixed_imag
    output_imag = filter_real * mixed_imag + filter_imag * mixed_real
    backward_real = filter_real * gated_real + filter_imag * gated_imag
    backward_imag = filter_real * gated_imag - filter_imag * gated_real
    kernel_real = mixed_real * gated_real + mixed_imag * gated_imag
    kernel_imag = mixed_real * gated_imag - mixed_imag * gated_real
    signals = inverse_real(
        jnp.concatenate((output_real, backward_real, kernel_real), 0),
        jnp.concatenate((output_imag, backward_imag, kernel_imag), 0),
        tables,
    )
    conv_out, conv_grad, filter_grad = jnp.split(signals.astype(jnp.bfloat16), 3, 0)
    return (conv_out, conv_grad, filter_grad)


def body(queries, key_input, value_input, basis_filters, tucker_factor, skip_bias, cotangent):
    seq_count = lax.axis_size("seq")
    seq_rank = lax.axis_index("seq")
    seq_rows = queries.shape[0]
    length = seq_rows * seq_count
    grad_scale = length ** (-0.5)
    tables = make_tables(length)
    mixed_in = (key_input.astype(jnp.float32) * value_input.astype(jnp.float32)).astype(
        jnp.bfloat16
    )
    mixed_in = lax.optimization_barrier(mixed_in)
    gated_grad = (cotangent.astype(jnp.float32) * queries.astype(jnp.float32)).astype(jnp.bfloat16)
    gated_grad = lax.optimization_barrier(gated_grad)
    mixed_cols = mixed_in.T
    gated_cols = gated_grad.T
    chan_local = queries.shape[1] // seq_count
    factor_rows = lax.dynamic_slice_in_dim(tucker_factor, seq_rank * chan_local, chan_local, 0)
    mixed_chan, gated_chan = (
        lax.all_to_all(mixed_cols, "seq", split_axis=0, concat_axis=1, tiled=True),
        lax.all_to_all(gated_cols, "seq", split_axis=0, concat_axis=1, tiled=True),
    )
    filter_chan = lax.dot_general(
        factor_rows,
        lax.all_gather(basis_filters, "seq", axis=0, tiled=True),
        (((1,), (1,)), ((), ())),
        preferred_element_type=jnp.float32,
    ).astype(jnp.bfloat16)
    conv_out, conv_grad, filter_grad = convolve(mixed_chan, gated_chan, filter_chan, tables)
    output_cols, backward_cols = (
        lax.all_to_all(as_sent(conv_out), "seq", split_axis=1, concat_axis=0, tiled=True).astype(
            conv_out.dtype
        ),
        lax.all_to_all(as_sent(conv_grad), "seq", split_axis=1, concat_axis=0, tiled=True).astype(
            conv_grad.dtype
        ),
    )
    zero_running = jnp.zeros((chan_local, basis_filters.shape[1]), jnp.float32)
    shard_rows = jax.tree.map(lambda a: lax.all_gather(a, "seq", axis=0, tiled=True), basis_filters)
    grad_taps = lax.slice_in_dim(filter_grad, 0, shard_rows.shape[0], axis=1)
    factor_part = zero_running + jnp.dot(grad_taps, shard_rows, preferred_element_type=jnp.float32)
    grad_factor = lax.all_gather(
        (factor_part * grad_scale).astype(jnp.bfloat16), "seq", axis=0, tiled=True
    ).astype(jnp.float32)
    grad_taps = lax.slice_in_dim(filter_grad, 0, lax.axis_size("seq") * seq_rows, axis=1)
    basis_part = lax.psum_scatter(
        lax.dot_general(
            grad_taps, factor_rows, (((0,), (0,)), ((), ())), preferred_element_type=jnp.float32
        ).astype(jnp.bfloat16),
        "seq",
        scatter_dimension=0,
        tiled=True,
    )
    grad_basis = lax.psum(basis_part, "chan").astype(jnp.float32) * grad_scale
    pre_gate = output_cols.T.astype(jnp.float32) + skip_bias * mixed_in.astype(jnp.float32)
    hyena_out = (queries.astype(jnp.float32) * pre_gate).astype(jnp.bfloat16)
    grad_query = (cotangent.astype(jnp.float32) * pre_gate).astype(jnp.bfloat16)
    grad_mixed = backward_cols.T.astype(jnp.float32) + skip_bias * gated_grad.astype(jnp.float32)
    grad_key = (grad_mixed * value_input.astype(jnp.float32)).astype(jnp.bfloat16)
    grad_value = (grad_mixed * key_input.astype(jnp.float32)).astype(jnp.bfloat16)
    return (hyena_out, grad_query, grad_key, grad_value, grad_factor, grad_basis)


def solution(mesh):
    return jax.shard_map(
        body,
        mesh=mesh,
        in_specs=(
            P("seq", "chan"),
            P("seq", "chan"),
            P("seq", "chan"),
            P("seq", None),
            P("chan", None),
            P("chan"),
            P("seq", "chan"),
        ),
        out_specs=(
            P("seq", "chan"),
            P("seq", "chan"),
            P("seq", "chan"),
            P("seq", "chan"),
            P("chan", None),
            P("seq", None),
        ),
        check_vma=False,
    )
```

profile of v0, /device:TPU:0, one launch (start us, length us, event | category | flops | bytes accessed | tf_op | source)
XLA Modules:
  0.0 706.0 jit_solution(17958207717143637112)
XLA Ops:
  7.9 3.2 fusion.27
  11.1 2.6 copy.39
  13.7 5.2 all-to-all-start.1
  18.9 4.7 fusion.25
  23.7 3.9 copy.37
  27.6 23.6 %all-to-all-done.1 = bf16[8,128,1024]{2,1,0:T(8,128)(2,1)} async-done(((bf16[8,128,1024]{2,1,0:T(8,128)(2,1)}), bf16[8,128,1024]{2,1,0:T(8,128)(2,1)}, u32[]{:S(2)}, u32[]{:S(2)}) %all-to-all-start.1) | async-done | bytes 2097184 | tf_op jit(solution)/shard_map/all_to_all | solution.py:126
  51.2 3.6 all-to-all-start
  55.9 4.2 copy.40
  60.1 4.7 concatenate.17
  64.8 22.9 %all-to-all-done = bf16[8,128,1024]{2,1,0:T(8,128)(2,1)S(1)} async-done(((bf16[8,128,1024]{2,1,0:T(8,128)(2,1)}), bf16[8,128,1024]{2,1,0:T(8,128)(2,1)S(1)}, u32[]{:S(2)}, u32[]{:S(2)}) %all-to-all-start) | async-done | bytes 2097184 | tf_op jit(solution)/shard_map/all_to_all | solution.py:125
  87.7 2.5 copy.38
  90.1 4.3 concatenate.16
  94.4 3.1 constant_dynamic-update-slice_fusion.2
  99.0 3.7 fusion.36
  104.8 12.0 %fusion.73 = f32[384,128,128]{2,1,0:T(8,128)} fusion(bf16[384,64,128]{2,1,0:T(8,128)(2,1)} %constant_dynamic-update-slice_fusion, f32[128,128]{0,1:T(8,128)S(1)} %get-tuple-element.26), kind=kOutput, calls=%fused_computation.103 | convolution fusion | flops 805339136 | bytes 31490048 | tf_op jit(solution)/shard_map/kn,cna->cka/dot_general | solution.py:47
  116.8 12.0 %fusion.80 = f32[384,128,128]{2,1,0:T(8,128)} fusion(bf16[384,64,128]{2,1,0:T(8,128)(2,1)} %constant_dynamic-update-slice_fusion, f32[128,128]{0,1:T(8,128)S(1)} %get-tuple-element.26), kind=kOutput, calls=%fused_computation.108 | convolution fusion | flops 805306368 | bytes 31473664 | tf_op jit(solution)/shard_map/kn,cna->cka/dot_general | solution.py:45
  128.8 12.1 %fusion.76 = f32[384,128,128]{2,1,0:T(8,128)} fusion(bf16[384,64,128]{2,1,0:T(8,128)(2,1)} %constant_dynamic-update-slice_fusion, f32[128,128]{0,1:T(8,128)S(1)} %get-tuple-element.24), kind=kOutput, calls=%fused_computation.105 | convolution fusion | flops 805339136 | bytes 31490048 | tf_op jit(solution)/shard_map/kn,cna->cka/dot_general | solution.py:47
  140.9 43.7 %fusion.1 = (f32[384,128,128]{1,2,0:T(8,128)}, f32[384,128,128]{1,2,0:T(8,128)}) fusion(f32[128,128]{0,1:T(8,128)S(1)} %get-tuple-element.23, f32[128,128]{0,1:T(8,128)S(1)} %get-tuple-element.25, f32[384,128,128]{2,1,0:T(8,128)} %fusion.76, f32[384,128,128]{2,1,0:T(8,128)} %fusion.80, f32[384,128,128]{2,1,0:T(8,128)} %fusion.73, ...), kind=kOutput, calls=%fused_computation.5 | convolution fusion | flops 855638016 | bytes 132268032 | tf_op jit(solution)/shard_map/kn,cna->cka/dot_general | solution.py:45
  184.6 27.3 %fusion.49 = f32[384,128,128]{2,1,0:T(8,128)} fusion(f32[384,128,128]{1,2,0:T(8,128)} %get-tuple-element.7), kind=kOutput, calls=%fused_computation.76 | convolution fusion | flops 4832083968 | bytes 50331648 | tf_op jit(solution)/shard_map/cka,ja->ckj/dot_general | solution.py:62
  211.9 27.3 %fusion.55 = f32[384,128,128]{2,1,0:T(8,128)} fusion(f32[384,128,128]{1,2,0:T(8,128)} %get-tuple-element.7), kind=kOutput, calls=%fused_computation.82 | convolution fusion | flops 4832067584 | bytes 50331648 | tf_op jit(solution)/shard_map/cka,ja->ckj/dot_general | solution.py:59
  239.2 34.1 %convolution_add_fusion = f32[384,128,128]{2,1,0:T(8,128)} fusion(f32[384,128,128]{2,1,0:T(8,128)} %fusion.49, f32[384,128,128]{1,2,0:T(8,128)} %get-tuple-element.6), kind=kOutput, calls=%fused_computation.31 | convolution fusion | flops 4838359040 | bytes 75497472 | tf_op jit(solution)/shard_map/cka,ja->ckj/dot_general | solution.py:64
  273.2 34.3 %convolution_subtract_fusion = f32[384,128,128]{2,1,0:T(8,128)} fusion(f32[384,128,128]{2,1,0:T(8,128)} %fusion.55, f32[384,128,128]{1,2,0:T(8,128)} %get-tuple-element.6), kind=kOutput, calls=%fused_computation.32 | convolution fusion | flops 4838375424 | bytes 75497472 | tf_op jit(solution)/shard_map/cka,ja->ckj/dot_general | solution.py:61
  307.6 24.6 %multiply_add_fusion.2 = (f32[128,128,128]{2,1,0:T(8,128)}, f32[128,128,128]{2,1,0:T(8,128)}) fusion(f32[384,128,128]{2,1,0:T(8,128)} %convolution_add_fusion, f32[384,128,128]{2,1,0:T(8,128)} %convolution_subtract_fusion), kind=kLoop, calls=%fused_computation.37 | loop fusion | flops 12582912 | bytes 67108864 | tf_op jit(solution)/shard_map/add | solution.py:94
  332.2 30.9 %multiply_subtract_fusion.2 = (f32[128,128,128]{2,1,0:T(8,128)}, f32[128,128,128]{2,1,0:T(8,128)}, f32[128,128,128]{2,1,0:T(8,128)}, f32[128,128,128]{2,1,0:T(8,128)}) fusion(f32[384,128,128]{2,1,0:T(8,128)} %convolution_add_fusion, f32[384,128,128]{2,1,0:T(8,128)} %convolution_subtract_fusion), kind=kLoop, calls=%fused_computation.38 | loop fusion | flops 25165824 | bytes 83886080 | tf_op jit(solution)/shard_map/sub | solution.py:92
  363.0 23.1 %fusion.12 = f32[384,128,128]{1,2,0:T(8,128)} fusion(f32[128,128,128]{2,1,0:T(8,128)} %get-tuple-element.9, f32[128,128,128]{2,1,0:T(8,128)} %get-tuple-element.12, f32[128,128,128]{2,1,0:T(8,128)} %get-tuple-element.8), kind=kOutput, calls=%fused_computation.18 | convolution fusion | flops 4844666880 | bytes 50331648 | tf_op jit(solution)/shard_map/ckj,aj->cka/dot_general | solution.py:77
  386.2 23.0 %fusion.13 = f32[384,128,128]{1,2,0:T(8,128)} fusion(f32[128,128,128]{2,1,0:T(8,128)} %get-tuple-element.9, f32[128,128,128]{2,1,0:T(8,128)} %get-tuple-element.12, f32[128,128,128]{2,1,0:T(8,128)} %get-tuple-element.8), kind=kOutput, calls=%fused_computation.19 | convolution fusion | flops 4844650496 | bytes 50331648 | tf_op jit(solution)/shard_map/ckj,aj->cka/dot_general | solution.py:72
  409.2 23.0 %fusion.10 = f32[384,128,128]{1,2,0:T(8,128)} fusion(f32[128,128,128]{2,1,0:T(8,128)} %get-tuple-element.11, f32[128,128,128]{2,1,0:T(8,128)} %get-tuple-element.10, f32[128,128,128]{2,1,0:T(8,128)} %get-tuple-element.13), kind=kOutput, calls=%fused_computation.16 | convolution fusion | flops 4844650496 | bytes 50331648 | tf_op jit(solution)/shard_map/ckj,aj->cka/dot_general | solution.py:75
  432.2 23.2 %fusion.11 = f32[384,128,128]{1,2,0:T(8,128)} fusion(f32[128,128,128]{2,1,0:T(8,128)} %get-tuple-element.11, f32[128,128,128]{2,1,0:T(8,128)} %get-tuple-element.10, f32[128,128,128]{2,1,0:T(8,128)} %get-tuple-element.13), kind=kOutput, calls=%fused_computation.17 | convolution fusion | flops 4844666880 | bytes 50331648 | tf_op jit(solution)/shard_map/ckj,aj->cka/dot_general | solution.py:74
  455.4 38.4 %fusion.2 = f32[384,128,64]{1,2,0:T(8,128)} fusion(f32[128,128]{0,1:T(8,128)S(1)} %copy-done.7, f32[128,128]{0,1:T(8,128)S(1)} %copy-done.5, f32[384,128,128]{1,2,0:T(8,128)} %fusion.10, f32[384,128,128]{1,2,0:T(8,128)} %fusion.12, f32[384,128,128]{1,2,0:T(8,128)} %fusion.13, f32[384,128,128]{1,2,0:T(8,128)} %fusion.11, f32[128,128]{0,1:T(8,128)S(1)} %copy-done.11), kind=kOutput, calls=%fused_computation.8 | convolution fusion | flops 2447376384 | bytes 113442816 | tf_op jit(solution)/shard_map/nk,cka->cna/dot_general | solution.py:82
  493.9 40.0 %fusion.22 = bf16[384,64,128]{2,1,0:T(8,128)(2,1)} fusion(f32[384,128,64]{1,2,0:T(8,128)} %fusion.2, f32[128,128]{0,1:T(8,128)S(1)} %copy-done.7, f32[128,128]{0,1:T(8,128)S(1)} %copy-done.5, f32[384,128,128]{1,2,0:T(8,128)} %fusion.10, f32[384,128,128]{1,2,0:T(8,128)} %fusion.12, f32[384,128,128]{1,2,0:T(8,128)} %fusion.13, f32[384,128,128]{1,2,0:T(8,128)} %fusion.11, ...), kind=kOutput, calls=%fused_computation.39 | convolution fusion | flops 2456813568 | bytes 119734272 | tf_op jit(solution)/shard_map/nk,cka->cna/dot_general | solution.py:80
  533.9 7.1 %fusion.120 = (bf16[128,64,128]{2,1,0:T(8,128)(2,1)S(1)}, bf16[128,64,128]{2,1,0:T(8,128)(2,1)}, bf16[128,64,128]{2,1,0:T(8,128)(2,1)}) fusion(bf16[384,64,128]{2,1,0:T(8,128)(2,1)} %fusion.22), kind=kLoop, calls=%fused_computation.151 | loop fusion | bytes 12582912 | tf_op jit(solution)/shard_map/split | solution.py:103
  541.0 5.1 convolution_convert_fusion
  546.1 4.2 all_to_all.52
  550.3 4.1 copy.63
  554.4 4.4 all-to-all-start.3
  558.8 4.2 all_to_all.50
  563.0 4.1 copy.61
  567.1 29.6 %all-to-all-done.3 = bf16[128,8,1024]{2,0,1:T(8,128)(2,1)} async-done(((bf16[128,8,1024]{2,0,1:T(8,128)(2,1)}), bf16[128,8,1024]{2,0,1:T(8,128)(2,1)}, u32[]{:S(2)}, u32[]{:S(2)}) %all-to-all-start.3) | async-done | bytes 2097184 | tf_op jit(solution)/shard_map/all_to_all | solution.py:139
  596.6 4.4 all-to-all-start.2
  601.0 3.9 fusion.40
  605.0 32.5 %all_gather.8 = bf16[1024,256]{1,0:T(8,128)(2,1)S(1)} all-gather(bf16[128,256]{1,0:T(8,128)(2,1)S(1)} %fusion.40), channel_id=1, replica_groups=mesh['seq'=8,'chan'=4] {'seq'}, dimensions={0}, use_global_device_ids=true | all-gather | bytes 589824 | tf_op jit(solution)/shard_map/all_gather | solution.py:147
  638.6 4.0 convert_element_type.202
  642.6 5.7 copy.64
  648.3 4.2 convert_element_type.201
  652.5 5.4 copy.62
  657.9 11.1 %fusion.24 = (bf16[1024,1024]{1,0:T(8,128)(2,1)}, bf16[1024,1024]{1,0:T(8,128)(2,1)}, bf16[1024,1024]{1,0:T(8,128)(2,1)}, bf16[1024,1024]{1,0:T(8,128)(2,1)}) fusion(bf16[1024,1024]{1,0:T(8,128)(2,1)} %param.8, bf16[1024,1024]{1,0:T(8,128)(2,1)S(1)} %copy-done.2, f32[1024,1024]{0,1:T(8,128)} %copy.64, f32[1024]{0:T(1024)S(1)} %copy-done.12, ...), kind=kLoop, calls=%fused_computation.47 | loop fusion | flops 18874368 | bytes 29364224 | tf_op jit(solution)/shard_map/convert_element_type | solution.py:165
  669.0 27.8 %all-reduce.2.cloned.1.call-done = bf16[1024,256]{1,0:T(8,128)(2,1)} async-done(((bf16[1024,256]{1,0:T(8,128)(2,1)}), bf16[1024,256]{1,0:T(8,128)(2,1)}) %all-reduce.2.cloned.1.call-update) | async-done | bytes 524304 | tf_op jit(solution)/shard_map/psum | solution.py:159
  696.8 2.1 convert_multiply_fusion.6
  (41 shorter events, 6.5 us)
Async XLA Ops:
  7.2 91.9 %copy-start = (bf16[1024,256]{1,0:T(8,128)(2,1)S(1)}, bf16[1024,256]{1,0:T(8,128)(2,1)}, u32[]{:S(2)}) copy-start(bf16[1024,256]{1,0:T(8,128)(2,1)} %param.11) | copy-start | bytes 1572868
  7.2 91.8 %all-gather.2.cloned.1.call-start = ((), (), s32[]{:S(2)}) async-start(), calls=%async_computation.5 | async-start | bytes 4718592 | tf_op jit(solution)/shard_map/all_gather | solution.py:130
  11.1 16.5 %copy-start.1 = (bf16[1024,1024]{1,0:T(8,128)(2,1)}, bf16[1024,1024]{1,0:T(8,128)(2,1)S(1)}, u32[]{:S(2)}) copy-start(bf16[1024,1024]{1,0:T(8,128)(2,1)S(1)} %fusion.27) | copy-start | bytes 6291460
  13.7 37.5 %all-to-all-start.1 = ((bf16[8,128,1024]{2,1,0:T(8,128)(2,1)}), bf16[8,128,1024]{2,1,0:T(8,128)(2,1)}, u32[]{:S(2)}, u32[]{:S(2)}) async-start(bf16[8,128,1024]{2,1,0:T(8,128)(2,1)} %bitcast.115), calls=%async_computation.1 | async-start | bytes 4194304 | tf_op jit(solution)/shard_map/all_to_all | solution.py:126
  51.2 36.4 %all-to-all-start = ((bf16[8,128,1024]{2,1,0:T(8,128)(2,1)}), bf16[8,128,1024]{2,1,0:T(8,128)(2,1)S(1)}, u32[]{:S(2)}, u32[]{:S(2)}) async-start(bf16[8,128,1024]{2,1,0:T(8,128)(2,1)} %bitcast.113), calls=%async_computation | async-start | bytes 4194304 | tf_op jit(solution)/shard_map/all_to_all | solution.py:125
  54.8 603.0 %reduce-scatter.2.cloned.1.call-start = ((), (), s32[]{:S(2)}) async-start(), calls=%async_computation.6 | async-start | bytes 4718592 | tf_op jit(solution)/shard_map/reduce_scatter | solution.py:151
  55.4 61.4 %copy-start.8 = (f32[128,128]{0,1:T(8,128)}, f32[128,128]{0,1:T(8,128)S(1)}, u32[]{:S(2)}) copy-start(f32[128,128]{0,1:T(8,128)S(1)} %get-tuple-element.26) | copy-start | bytes 196612
  55.4 85.5 %copy-start.4 = (f32[128,128]{0,1:T(8,128)}, f32[128,128]{0,1:T(8,128)S(1)}, u32[]{:S(2)}) copy-start(f32[128,128]{0,1:T(8,128)S(1)} %get-tuple-element.25) | copy-start | bytes 196612
  55.9 85.0 %copy-start.6 = (f32[128,128]{0,1:T(8,128)}, f32[128,128]{0,1:T(8,128)S(1)}, u32[]{:S(2)}) copy-start(f32[128,128]{0,1:T(8,128)S(1)} %get-tuple-element.23) | copy-start | bytes 196612
  55.9 84.9 %copy-start.10 = (f32[128,128]{0,1:T(8,128)}, f32[128,128]{0,1:T(8,128)S(1)}, u32[]{:S(2)}) copy-start(f32[128,128]{0,1:T(8,128)S(1)} %get-tuple-element.24) | copy-start | bytes 196612
  90.1 7.4 %copy-start.3 = (bf16[128,64,128]{2,1,0:T(8,128)(2,1)S(1)}, bf16[128,64,128]{2,1,0:T(8,128)(2,1)}, u32[]{:S(2)}) copy-start(bf16[128,64,128]{2,1,0:T(8,128)(2,1)} %concatenate.17) | copy-start | bytes 6291460
  432.1 23.2 %copy-start.5 = (f32[128,128]{0,1:T(8,128)S(1)}, f32[128,128]{0,1:T(8,128)}, u32[]{:S(2)}) copy-start(f32[128,128]{0,1:T(8,128)} %copy-done.4) | copy-start | bytes 196612
  432.2 23.2 %copy-start.7 = (f32[128,128]{0,1:T(8,128)S(1)}, f32[128,128]{0,1:T(8,128)}, u32[]{:S(2)}) copy-start(f32[128,128]{0,1:T(8,128)} %copy-done.6) | copy-start | bytes 196612
  432.2 23.2 %copy-start.11 = (f32[128,128]{0,1:T(8,128)S(1)}, f32[128,128]{0,1:T(8,128)}, u32[]{:S(2)}) copy-start(f32[128,128]{0,1:T(8,128)} %copy-done.10) | copy-start | bytes 196612
  455.4 38.5 %copy-start.9 = (f32[128,128]{0,1:T(8,128)S(1)}, f32[128,128]{0,1:T(8,128)}, u32[]{:S(2)}) copy-start(f32[128,128]{0,1:T(8,128)} %copy-done.8) | copy-start | bytes 196612
  554.4 42.2 %all-to-all-start.3 = ((bf16[128,8,1024]{2,0,1:T(8,128)(2,1)}), bf16[128,8,1024]{2,0,1:T(8,128)(2,1)}, u32[]{:S(2)}, u32[]{:S(2)}) async-start(bf16[128,8,1024]{2,0,1:T(8,128)(2,1)} %copy.63), calls=%async_computation.3 | async-start | bytes 4194304 | tf_op jit(solution)/shard_map/all_to_all | solution.py:139
  596.6 51.7 %all-to-all-start.2 = ((bf16[128,8,1024]{2,0,1:T(8,128)(2,1)}), bf16[128,8,1024]{2,0,1:T(8,128)(2,1)}, u32[]{:S(2)}, u32[]{:S(2)}) async-start(bf16[128,8,1024]{2,0,1:T(8,128)(2,1)} %copy.61), calls=%async_computation.2 | async-start | bytes 4194304 | tf_op jit(solution)/shard_map/all_to_all | solution.py:136
  601.0 95.8 %all-reduce.2.cloned.1.call-start = ((), (), s32[]{:S(2)}) async-start(), calls=%async_computation.7 | async-start | bytes 1048576 | tf_op jit(solution)/shard_map/psum | solution.py:159
  648.3 9.6 %copy-start.2 = (bf16[1024,1024]{1,0:T(8,128)(2,1)S(1)}, bf16[1024,1024]{1,0:T(8,128)(2,1)}, u32[]{:S(2)}) copy-start(bf16[1024,1024]{1,0:T(8,128)(2,1)} %copy-done.1) | copy-start | bytes 6291460
  648.3 9.6 %copy-start.12 = (f32[1024]{0:T(1024)S(1)}, f32[1024]{0:T(1024)}, u32[]{:S(2)}) copy-start(f32[1024]{0:T(1024)} %param.12) | copy-start | bytes 12292
Sparse Core Ops, SparseCore 0:
  9.9 62.5 all-gather.1
  546.2 71.4 reduce-scatter.1
  658.0 38.7 all-reduce.1
where the time goes:
time: 712 us; the launch traced here: 706 us
  matrix products  386 us (54%)
  waiting for transfers between devices  105 us (15%)
  other arithmetic  86.9 us (12%)
  local copies, waits for them, and re-layouts  63.7 us (9%)
  blocking collectives  32.5 us (5%)
  starting transfers between devices  17.7 us (2%)
  between operations  14.4 us (2%)
    dot_general x2, matrix products, table_product(): jnp.einsum('kn,cna->cka', high_part, blocks, preferred_element_type=jnp.f...  55.7 us
    dot_general x1, matrix products, inverse_real(): jnp.einsum('nk,cka->cna', cosine_outer[:outer_half], twist_real, precisio...  40 us
    dot_general x1, matrix products, inverse_real(): jnp.einsum('nk,cka->cna', sine_outer[:outer_half], twist_imag, precision=...  38.4 us
    dot_general x1, matrix products, forward_real(): jnp.einsum('cka,ja->ckj', twist_imag, sine_inner, precision=ACCURATE)  34.3 us
    dot_general x1, matrix products, forward_real(): jnp.einsum('cka,ja->ckj', twist_imag, cosine_inner, precision=ACCURATE)  34.1 us
    all_gather x1, blocking collectives, body(): lax.all_gather((factor_part * grad_scale).astype(jnp.bfloat16), 'seq', ax...  32.5 us
    sub x1, other arithmetic, convolve(): output_real = filter_real * mixed_real - filter_imag * mixed_imag  30.9 us
    all_to_all x1, waiting for transfers between devices, body(): lax.all_to_all(as_sent(conv_grad), 'seq', split_axis=1, concat_axis=0, ti...  29.6 us
  transfers between devices with their start and end apart: 7, of which 4 were waited for; matrix products, arithmetic and copies ran while one was open for 11% of the time, Pallas kernels for 0%

commit v1 on v0

--- a/solution.py
+++ b/solution.py
@@ -3,13 +3,11 @@
 import jax
 import jax.numpy as jnp
 from jax import lax
+from jax.experimental import pallas as pl
+from jax.experimental.pallas import tpu as pltpu
 from jax.sharding import PartitionSpec as P
 
 ACCURATE = lax.Precision.HIGH
-
-
-def as_sent(shard):
-    return jax.tree.map(lambda a: a.astype(jnp.bfloat16) if a.dtype == jnp.float32 else a, shard)
 
 
 def split_length(length):
@@ -104,63 +102,223 @@
     return (conv_out, conv_grad, filter_grad)
 
 
+LANES = 128
+
+
+def split_table(table, axis):
+    high_part = table.astype(jnp.bfloat16)
+    low_part = (table - high_part.astype(jnp.float32)).astype(jnp.bfloat16)
+    return jnp.concatenate((high_part, low_part), axis)
+
+
+def angle_table(left, right, period):
+    product = left[:, None] * right[None, :] % period
+    return product.astype(jnp.float32) * (2.0 * math.pi / period)
+
+
+def kernel_tables(length):
+    half = length // LANES
+    padded_size = 2 * length
+    odd = 2 * jnp.arange(half, dtype=jnp.int32) + 1
+    rows = jnp.arange(half, dtype=jnp.int32)
+    lags = jnp.arange(LANES, dtype=jnp.int32)
+    outer = angle_table(odd, rows, 4 * half)
+    first = split_table(jnp.concatenate((jnp.cos(outer), -jnp.sin(outer)), 0), 1)
+    last = jnp.concatenate((jnp.cos(outer), -jnp.sin(outer)), 0).T * (2.0 / padded_size)
+    inner = angle_table(lags, lags, LANES)
+    twist = angle_table(odd, lags, 2 * padded_size)
+    return (
+        first,
+        split_table(last, 1),
+        jnp.cos(inner),
+        jnp.sin(inner),
+        jnp.cos(twist)[:, None, :],
+        jnp.sin(twist)[:, None, :],
+    )
+
+
+def conv_kernel(mixed, gated, taps, first, last, cosine, sine, tw_cos, tw_sin, *rest):
+    outs, (held, spec) = rest[:3], rest[3:]
+    sources = (mixed, gated, taps)
+    half = mixed.shape[0] // LANES
+    pitch = LANES + 8
+
+    def widen(j, carry):
+        for g in range(3):
+            rows = sources[g][pl.ds(pl.multiple_of(j * LANES, LANES), LANES), :]
+            held[g, pl.ds(pl.multiple_of(j * pitch, 8), LANES), :] = rows.astype(jnp.float32)
+        return carry
+
+    lax.fori_loop(0, half, widen, 0)
+    first_table = first[...]
+
+    def analyse(i, carry):
+        for g in range(3):
+            pair = jnp.concatenate(
+                [held[g, pl.ds(2 * i + e, half, stride=pitch), :] for e in range(2)], 1
+            ).astype(jnp.bfloat16)
+            section = jnp.dot(
+                first_table,
+                jnp.concatenate((pair, pair), 0),
+                preferred_element_type=jnp.float32,
+            )
+            for e in range(2):
+                spec[g, pl.ds(2 * i + e, 2 * half, stride=pitch), :] = section[
+                    :, e * LANES : (e + 1) * LANES
+                ]
+        return carry
+
+    lax.fori_loop(0, LANES // 2, analyse, 0, unroll=2)
+
+    def multiply(k, carry):
+        real_rows = pl.ds(pl.multiple_of(k * pitch, 8), LANES)
+        imag_rows = pl.ds(pl.multiple_of((half + k) * pitch, 8), LANES)
+        real = cosine[...] * tw_cos[k] - sine[...] * tw_sin[k]
+        imag = -(sine[...] * tw_cos[k] + cosine[...] * tw_sin[k])
+        forward = jnp.concatenate(
+            (jnp.concatenate((real, -imag), 1), jnp.concatenate((imag, real), 1)), 0
+        ).astype(jnp.bfloat16)
+        real, imag = real.T, imag.T
+        backward = jnp.concatenate(
+            (jnp.concatenate((real, imag), 1), jnp.concatenate((-imag, real), 1)), 0
+        ).astype(jnp.bfloat16)
+        section = jnp.concatenate(
+            [
+                jnp.concatenate((spec[g, real_rows, :], spec[g, imag_rows, :]), 0)
+                for g in range(3)
+            ],
+            1,
+        ).astype(jnp.bfloat16)
+        spectrum = jnp.dot(forward, section, preferred_element_type=jnp.float32)
+        mr, gr, fr = (spectrum[:LANES, g * LANES : (g + 1) * LANES] for g in range(3))
+        mi, gi, fi = (spectrum[LANES:, g * LANES : (g + 1) * LANES] for g in range(3))
+        product = jnp.concatenate(
+            (
+                jnp.concatenate((fr * mr - fi * mi, fr * gr + fi * gi, mr * gr + mi * gi), 1),
+                jnp.concatenate((fr * mi + fi * mr, fr * gi - fi * gr, mr * gi - mi * gr), 1),
+            ),
+            0,
+        ).astype(jnp.bfloat16)
+        result = jnp.dot(backward, product, preferred_element_type=jnp.float32)
+        for g in range(3):
+            spec[g, real_rows, :] = result[:LANES, g * LANES : (g + 1) * LANES]
+            spec[g, imag_rows, :] = result[LANES:, g * LANES : (g + 1) * LANES]
+        return carry
+
+    lax.fori_loop(0, half, multiply, 0, unroll=2)
+    last_table = last[...]
+
+    def synthesise(i, carry):
+        for g in range(3):
+            pair = jnp.concatenate(
+                [spec[g, pl.ds(2 * i + e, 2 * half, stride=pitch), :] for e in range(2)], 1
+            ).astype(jnp.bfloat16)
+            signal = jnp.dot(
+                last_table,
+                jnp.concatenate((pair, pair), 0),
+                preferred_element_type=jnp.float32,
+            )
+            for e in range(2):
+                held[g, pl.ds(2 * i + e, half, stride=pitch), :] = signal[
+                    :, e * LANES : (e + 1) * LANES
+                ]
+        return carry
+
+    lax.fori_loop(0, LANES // 2, synthesise, 0, unroll=2)
+
+    def narrow(j, carry):
+        for g in range(3):
+            rows = held[g, pl.ds(pl.multiple_of(j * pitch, 8), LANES), :]
+            outs[g][pl.ds(pl.multiple_of(j * LANES, LANES), LANES), :] = rows.astype(jnp.bfloat16)
+        return carry
+
+    lax.fori_loop(0, half, narrow, 0)
+
+
+def convolve_lanes(mixed, gated, taps):
+    length = mixed.shape[0]
+    half = length // LANES
+    pitch = LANES + 8
+    vmem = pl.BlockSpec(memory_space=pltpu.VMEM)
+    return pl.pallas_call(
+        conv_kernel,
+        out_shape=[jax.ShapeDtypeStruct(mixed.shape, jnp.bfloat16)] * 3,
+        in_specs=[vmem] * 9,
+        out_specs=[vmem] * 3,
+        scratch_shapes=[
+            pltpu.VMEM((3, half * pitch, LANES), jnp.float32),
+            pltpu.VMEM((3, 2 * half * pitch, LANES), jnp.float32),
+        ],
+        compiler_params=pltpu.CompilerParams(vmem_limit_bytes=60 * 1024 * 1024),
+    )(mixed, gated, taps, *kernel_tables(length))
+
+
+def convolve_any(mixed, gated, taps):
+    length, chans = mixed.shape
+    if chans == LANES and length == 64 * LANES:
+        return convolve_lanes(mixed, gated, taps)
+    outs = convolve(mixed.T, gated.T, taps.T, make_tables(length))
+    return tuple(out.T for out in outs)
+
+
+def to_blocks(matrix, count):
+    rows, cols = matrix.shape
+    return matrix.reshape(rows, count, cols // count).transpose(1, 0, 2)
+
+
+def from_blocks(blocks):
+    count, rows, cols = blocks.shape
+    return blocks.transpose(1, 0, 2).reshape(rows, count * cols)
+
+
 def body(queries, key_input, value_input, basis_filters, tucker_factor, skip_bias, cotangent):
     seq_count = lax.axis_size("seq")
     seq_rank = lax.axis_index("seq")
     seq_rows = queries.shape[0]
     length = seq_rows * seq_count
     grad_scale = length ** (-0.5)
-    tables = make_tables(length)
+    chan_local = queries.shape[1] // seq_count
+    basis_all = lax.all_gather(basis_filters, "seq", axis=0, tiled=True)
     mixed_in = (key_input.astype(jnp.float32) * value_input.astype(jnp.float32)).astype(
         jnp.bfloat16
     )
-    mixed_in = lax.optimization_barrier(mixed_in)
     gated_grad = (cotangent.astype(jnp.float32) * queries.astype(jnp.float32)).astype(jnp.bfloat16)
-    gated_grad = lax.optimization_barrier(gated_grad)
-    mixed_cols = mixed_in.T
-    gated_cols = gated_grad.T
-    chan_local = queries.shape[1] // seq_count
+    mixed_chan, gated_chan = (
+        lax.all_to_all(to_blocks(signal, seq_count), "seq", split_axis=0, concat_axis=0).reshape(
+            length, chan_local
+        )
+        for signal in (mixed_in, gated_grad)
+    )
     factor_rows = lax.dynamic_slice_in_dim(tucker_factor, seq_rank * chan_local, chan_local, 0)
-    mixed_chan, gated_chan = (
-        lax.all_to_all(mixed_cols, "seq", split_axis=0, concat_axis=1, tiled=True),
-        lax.all_to_all(gated_cols, "seq", split_axis=0, concat_axis=1, tiled=True),
-    )
     filter_chan = lax.dot_general(
-        factor_rows,
-        lax.all_gather(basis_filters, "seq", axis=0, tiled=True),
-        (((1,), (1,)), ((), ())),
-        preferred_element_type=jnp.float32,
+        basis_all, factor_rows, (((1,), (1,)), ((), ())), preferred_element_type=jnp.float32
     ).astype(jnp.bfloat16)
-    conv_out, conv_grad, filter_grad = convolve(mixed_chan, gated_chan, filter_chan, tables)
+    conv_out, conv_grad, filter_grad = convolve_any(mixed_chan, gated_chan, filter_chan)
+    basis_part = lax.psum_scatter(
+        jnp.dot(filter_grad, factor_rows, preferred_element_type=jnp.float32).astype(jnp.bfloat16),
+        "seq",
+        scatter_dimension=0,
+        tiled=True,
+    )
     output_cols, backward_cols = (
-        lax.all_to_all(as_sent(conv_out), "seq", split_axis=1, concat_axis=0, tiled=True).astype(
-            conv_out.dtype
-        ),
-        lax.all_to_all(as_sent(conv_grad), "seq", split_axis=1, concat_axis=0, tiled=True).astype(
-            conv_grad.dtype
-        ),
-    )
-    zero_running = jnp.zeros((chan_local, basis_filters.shape[1]), jnp.float32)
-    shard_rows = jax.tree.map(lambda a: lax.all_gather(a, "seq", axis=0, tiled=True), basis_filters)
-    grad_taps = lax.slice_in_dim(filter_grad, 0, shard_rows.shape[0], axis=1)
-    factor_part = zero_running + jnp.dot(grad_taps, shard_rows, preferred_element_type=jnp.float32)
+        from_blocks(
+            lax.all_to_all(
+                signal.reshape(seq_count, seq_rows, chan_local), "seq", split_axis=0, concat_axis=0
+            )
+        )
+        for signal in (conv_out, conv_grad)
+    )
+    factor_part = lax.dot_general(
+        filter_grad, basis_all, (((0,), (0,)), ((), ())), preferred_element_type=jnp.float32
+    )
     grad_factor = lax.all_gather(
         (factor_part * grad_scale).astype(jnp.bfloat16), "seq", axis=0, tiled=True
     ).astype(jnp.float32)
-    grad_taps = lax.slice_in_dim(filter_grad, 0, lax.axis_size("seq") * seq_rows, axis=1)
-    basis_part = lax.psum_scatter(
-        lax.dot_general(
-            grad_taps, factor_rows, (((0,), (0,)), ((), ())), preferred_element_type=jnp.float32
-        ).astype(jnp.bfloat16),
-        "seq",
-        scatter_dimension=0,
-        tiled=True,
-    )
     grad_basis = lax.psum(basis_part, "chan").astype(jnp.float32) * grad_scale
-    pre_gate = output_cols.T.astype(jnp.float32) + skip_bias * mixed_in.astype(jnp.float32)
+    pre_gate = output_cols.astype(jnp.float32) + skip_bias * mixed_in.astype(jnp.float32)
     hyena_out = (queries.astype(jnp.float32) * pre_gate).astype(jnp.bfloat16)
     grad_query = (cotangent.astype(jnp.float32) * pre_gate).astype(jnp.bfloat16)
-    grad_mixed = backward_cols.T.astype(jnp.float32) + skip_bias * gated_grad.astype(jnp.float32)
+    grad_mixed = backward_cols.astype(jnp.float32) + skip_bias * gated_grad.astype(jnp.float32)
     grad_key = (grad_mixed * value_input.astype(jnp.float32)).astype(jnp.bfloat16)
     grad_value = (grad_mixed * key_input.astype(jnp.float32)).astype(jnp.bfloat16)
     return (hyena_out, grad_query, grad_key, grad_value, grad_factor, grad_basis)

time: 712 us -> 267 us (0.38)
  matrix products: 386 us -> 12.8 us
  other arithmetic: 86.9 us -> 23.4 us
  local copies, waits for them, and re-layouts: 63.7 us -> 2.32 us
  Pallas kernels: 0 us -> 49.7 us
  blocking collectives: 32.5 us -> 70 us
  waiting for transfers between devices: 105 us -> 79.8 us
    dot_general x17 -> x3, matrix products: 386 us -> 12.8 us  [the longest x1 4.83 us: body(): jnp.dot(filter_grad, factor_rows, preferred_element_type=jnp.float32)]
    pallas_call x0 -> x1, Pallas kernels: none -> 49.7 us  [convolve_lanes(): pl.pallas_call(conv_kernel, out_shape=[jax.ShapeDtypeStruct(mixed.shape,...]
    all_to_all x0 -> x1, blocking collectives: none -> 36.7 us  [body(): lax.all_to_all(signal.reshape(seq_count, seq_rows, chan_local), 'seq', sp...]
    all_to_all x4 -> x3, waiting for transfers between devices: 76 us -> 42.9 us  [the longest x2 42.9 us: body(): lax.all_to_all(to_blocks(signal, seq_count), 'seq', split_axis=0, concat_...]
    sub x1 -> x0, other arithmetic: 30.9 us -> none  [convolve(): output_real = filter_real * mixed_real - filter_imag * mixed_imag]
    add x1, other arithmetic: 24.6 us -> 0.01 us  [kernel_tables(): odd = 2 * jnp.arange(half, dtype=jnp.int32) + 1]
    all_to_all x6 -> x0, local copies, waits for them, and re-layouts: 23.3 us -> none  [the longest x2 8.33 us: body(): lax.all_to_all(as_sent(conv_grad), 'seq', split_axis=1, concat_axis=0, ti...]
    convert_element_type x5, other arithmetic: 27.3 us -> 8.7 us  [the longest x1 8.52 us: body(): grad_query = (cotangent.astype(jnp.float32) * pre_gate).astype(jnp.bfloat16)]
  transfers between devices with their start and end apart: 7 -> 6, of which waited for: 4 -> 4; matrix products, arithmetic and copies ran while one was open for 11% -> 11% of each run, Pallas kernels for 0% -> 0%
where the time goes in v1:
time: 267 us; the launch traced here: 266 us
  waiting for transfers between devices  79.8 us (30%)
  blocking collectives  70 us (26%)
  Pallas kernels  49.7 us (19%)
  other arithmetic  23.4 us (9%)
  starting transfers between devices  14.2 us (5%)
  between operations  13.9 us (5%)
  matrix products  12.8 us (5%)
    pallas_call x1, Pallas kernels, convolve_lanes(): pl.pallas_call(conv_kernel, out_shape=[jax.ShapeDtypeStruct(mixed.shape,...  49.7 us
    all_to_all x2, waiting for transfers between devices, body(): lax.all_to_all(to_blocks(signal, seq_count), 'seq', split_axis=0, concat_...  42.9 us
    all_to_all x1, blocking collectives, body(): lax.all_to_all(signal.reshape(seq_count, seq_rows, chan_local), 'seq', sp...  36.7 us
    all_gather x1, blocking collectives, body(): lax.all_gather((factor_part * grad_scale).astype(jnp.bfloat16), 'seq', ax...  33.3 us
    psum x1, waiting for transfers between devices, body(): grad_basis = lax.psum(basis_part, 'chan').astype(jnp.float32) * grad_scale  30.7 us
    all_to_all x2, starting transfers between devices, body(): lax.all_to_all(to_blocks(signal, seq_count), 'seq', split_axis=0, concat_...  9.57 us
    convert_element_type x1, other arithmetic, body(): grad_query = (cotangent.astype(jnp.float32) * pre_gate).astype(jnp.bfloat16)  8.52 us
    transpose x2, other arithmetic, to_blocks(): return matrix.reshape(rows, count, cols // count).transpose(1, 0, 2)  8.31 us
  transfers between devices with their start and end apart: 6, of which 4 were waited for; matrix products, arithmetic and copies ran while one was open for 11% of the time, Pallas kernels for 0%

profile of v1, /device:TPU:0, one launch (start us, length us, event | category | flops | bytes accessed | tf_op | source)
XLA Modules:
  0.0 266.0 jit_solution(3154405724231390413)
XLA Ops:
  7.2 0.0 copy-start
  7.2 0.0 all-gather.2.cloned.1.call-start
  7.2 0.7 all-gather.2.cloned.1.call-update
  7.9 4.1 %bitcast_bitcast_fusion = bf16[8,1024,128]{2,1,0:T(8,128)(2,1)} fusion(bf16[1024,1024]{1,0:T(8,128)(2,1)} %param.7, bf16[1024,1024]{1,0:T(8,128)(2,1)} %param.13), kind=kLoop, calls=%fused_computation.19 | loop fusion | flops 4194304 | bytes 6291456 | tf_op jit(solution)/shard_map/transpose | solution.py:266
  12.0 5.2 %all-to-all-start.1 = ((bf16[8,1024,128]{2,1,0:T(8,128)(2,1)}), bf16[8,1024,128]{2,1,0:T(8,128)(2,1)S(1)}, u32[]{:S(2)}, u32[]{:S(2)}) async-start(bf16[8,1024,128]{2,1,0:T(8,128)(2,1)} %bitcast_bitcast_fusion), calls=%async_computation.1 | async-start | bytes 4194304 | tf_op jit(solution)/shard_map/all_to_all | solution.py:287
  17.2 4.2 %bitcast_bitcast_fusion.1 = bf16[8,1024,128]{2,1,0:T(8,128)(2,1)} fusion(bf16[1024,1024]{1,0:T(8,128)(2,1)} %param.9, bf16[1024,1024]{1,0:T(8,128)(2,1)} %param.8), kind=kLoop, calls=%fused_computation.20 | loop fusion | flops 4194304 | bytes 6291456 | tf_op jit(solution)/shard_map/transpose | solution.py:266
  21.4 29.1 %all-to-all-done.1 = bf16[8,1024,128]{2,1,0:T(8,128)(2,1)S(1)} async-done(((bf16[8,1024,128]{2,1,0:T(8,128)(2,1)}), bf16[8,1024,128]{2,1,0:T(8,128)(2,1)S(1)}, u32[]{:S(2)}, u32[]{:S(2)}) %all-to-all-start.1) | async-done | bytes 2097184 | tf_op jit(solution)/shard_map/all_to_all | solution.py:287
  50.6 0.0 copy-start.2
  50.6 4.4 %all-to-all-start = ((bf16[8,1024,128]{2,1,0:T(8,128)(2,1)}), bf16[8,1024,128]{2,1,0:T(8,128)(2,1)}, u32[]{:S(2)}, u32[]{:S(2)}) async-start(bf16[8,1024,128]{2,1,0:T(8,128)(2,1)} %bitcast_bitcast_fusion.1), calls=%async_computation | async-start | bytes 4194304 | tf_op jit(solution)/shard_map/all_to_all | solution.py:287
  54.9 0.0 reduce-scatter.2.cloned.1.call-start
  55.0 0.2 fusion.30
  55.1 0.0 copy-done.2
  55.2 0.1 bitcast_convert_fusion
  55.3 0.7 copy.23.first
  56.0 0.6 pad_maximum_fusion.2.last
  56.6 0.9 fusion.24
  57.5 0.1 fusion.20
  57.6 1.6 multiply_sine_fusion
  59.2 5.5 %all-gather.2.cloned.1.call-done = bf16[8192,256]{1,0:T(8,128)(2,1)} async-done(((bf16[1024,256]{1,0:T(8,128)(2,1)}), bf16[8192,256]{1,0:T(8,128)(2,1)}) %all-gather.2.cloned.1.call-update) | async-done | bytes 4194320 | tf_op jit(solution)/shard_map/all_gather | solution.py:281
  64.7 0.0 copy-done
  64.7 4.8 %fusion.taps = bf16[8192,128]{1,0:T(8,128)(2,1)} fusion(bf16[8192,256]{1,0:T(8,128)(2,1)} %all-gather.2.cloned.1.call-done, bf16[1024,256]{1,0:T(8,128)(2,1)S(1)} %copy-done, s32[]{:T(128)S(6)} %select_n.39), kind=kOutput, calls=%fused_computation.2 | convolution fusion | flops 537919488 | bytes 6356996 | tf_op jit(solution)/shard_map/dot_general | solution.py:293
  69.4 13.8 %all-to-all-done = bf16[8,1024,128]{2,1,0:T(8,128)(2,1)} async-done(((bf16[8,1024,128]{2,1,0:T(8,128)(2,1)}), bf16[8,1024,128]{2,1,0:T(8,128)(2,1)}, u32[]{:S(2)}, u32[]{:S(2)}) %all-to-all-start) | async-done | bytes 2097184 | tf_op jit(solution)/shard_map/all_to_all | solution.py:287
  83.3 49.7 %shard_map.118 = (bf16[8192,128]{1,0:T(8,128)(2,1)}, bf16[8192,128]{1,0:T(8,128)(2,1)}, bf16[8192,128]{1,0:T(8,128)(2,1)}) custom-call(bf16[8192,128]{1,0:T(8,128)(2,1)} %bitcast.1.mixed, bf16[8192,128]{1,0:T(8,128)(2,1)} %bitcast.52, bf16[8192,128]{1,0:T(8,128)(2,1)} %fusion.taps, bf16[128,128]{1,0:T(8,128)(2,1)} %copy.23.first, ...), custom_call_target="tpu_custom_call" | custom-call | tf_op jit(solution)/shard_map/pallas_call | solution.py:243
  132.9 4.8 %convolution_convert_fusion = bf16[8192,256]{1,0:T(8,128)(2,1)} fusion(bf16[8192,128]{1,0:T(8,128)(2,1)} %get-tuple-element.11, bf16[1024,256]{1,0:T(8,128)(2,1)S(1)} %copy-done, s32[]{:T(128)S(6)} %select_n.39), kind=kOutput, calls=%fused_computation | convolution fusion | flops 538968064 | bytes 6356996 | tf_op jit(solution)/shard_map/dot_general | solution.py:298
  137.7 0.0 copy-start.4
  137.7 0.0 reduce-scatter.2.cloned.1.call-update
  137.8 1.6 copy-done.4
  139.3 36.7 %all_to_all.20 = bf16[8,1024,128]{2,1,0:T(8,128)(2,1)} all-to-all(bf16[8,1024,128]{2,1,0:T(8,128)(2,1)S(1)} %bitcast.54), channel_id=1, replica_groups=mesh['seq'=8,'chan'=4] {'seq'}, dimensions={0} | all-to-all | bytes 4194304 | tf_op jit(solution)/shard_map/all_to_all | solution.py:305
  176.1 0.0 copy-start.1
  176.1 4.5 %all-to-all-start.2 = ((bf16[8,1024,128]{2,1,0:T(8,128)(2,1)}), bf16[8,1024,128]{2,1,0:T(8,128)(2,1)}, u32[]{:S(2)}, u32[]{:S(2)}) async-start(bf16[8,1024,128]{2,1,0:T(8,128)(2,1)} %bitcast.53), calls=%async_computation.2 | async-start | bytes 4194304 | tf_op jit(solution)/shard_map/all_to_all | solution.py:305
  180.6 0.0 all-reduce.2.cloned.1.call-start
  180.6 0.0 copy-done.1
  180.6 3.2 %fusion.7 = bf16[128,256]{1,0:T(8,128)(2,1)S(1)} fusion(bf16[8192,128]{1,0:T(8,128)(2,1)S(1)} %copy-done.1, bf16[8192,256]{1,0:T(8,128)(2,1)} %all-gather.2.cloned.1.call-done), kind=kOutput, calls=%fused_computation.22 | convolution fusion | flops 536936448 | bytes 6356992 | tf_op jit(solution)/shard_map/dot_general | solution.py:311
  183.8 0.0 copy-start.3
  183.8 0.0 copy-start.5
  183.8 33.3 %all_gather.7 = bf16[1024,256]{1,0:T(8,128)(2,1)S(1)} all-gather(bf16[128,256]{1,0:T(8,128)(2,1)S(1)} %fusion.7), channel_id=1, replica_groups=mesh['seq'=8,'chan'=4] {'seq'}, dimensions={0}, use_global_device_ids=true | all-gather | bytes 589824 | tf_op jit(solution)/shard_map/all_gather | solution.py:314
  217.1 1.0 convert_element_type.149
  218.1 0.0 reduce-scatter.2.cloned.1.call-done
  218.1 0.0 all-reduce.2.cloned.1.call-update
  218.2 0.0 all-to-all-done.2
  218.2 0.0 copy-done.3
  218.2 0.0 copy-done.5
  218.2 8.5 %fusion.6 = (bf16[1024,1024]{1,0:T(8,128)(2,1)}, bf16[1024,1024]{1,0:T(8,128)(2,1)}, bf16[1024,1024]{1,0:T(8,128)(2,1)}, bf16[1024,1024]{1,0:T(8,128)(2,1)}) fusion(bf16[1024,1024]{1,0:T(8,128)(2,1)S(1)} %copy-done.3, f32[1024]{0:T(1024)S(1)} %copy-done.5, bf16[1024,1024]{1,0:T(8,128)(2,1)} %param.9, bf16[1024,1024]{1,0:T(8,128)(2,1)} %param.8, ...), kind=kLoop, calls=%fused_computation.14 | loop fusion | flops 25165824 | bytes 20975616 | tf_op jit(solution)/shard_map/convert_element_type | solution.py:320
  226.7 30.7 %all-reduce.2.cloned.1.call-done = bf16[1024,256]{1,0:T(8,128)(2,1)} async-done(((bf16[1024,256]{1,0:T(8,128)(2,1)}), bf16[1024,256]{1,0:T(8,128)(2,1)}) %all-reduce.2.cloned.1.call-update) | async-done | bytes 524304 | tf_op jit(solution)/shard_map/psum | solution.py:317
  257.4 2.1 convert_multiply_fusion.6
  (4 shorter events, 0.0 us)
Async XLA Ops:
  7.2 57.5 %copy-start = (bf16[1024,256]{1,0:T(8,128)(2,1)S(1)}, bf16[1024,256]{1,0:T(8,128)(2,1)}, u32[]{:S(2)}) copy-start(bf16[1024,256]{1,0:T(8,128)(2,1)} %param.11) | copy-start | bytes 1572868
  7.2 57.5 %all-gather.2.cloned.1.call-start = ((), (), s32[]{:S(2)}) async-start(), calls=%async_computation.5 | async-start | bytes 4718592 | tf_op jit(solution)/shard_map/all_gather | solution.py:281
  12.0 38.5 %all-to-all-start.1 = ((bf16[8,1024,128]{2,1,0:T(8,128)(2,1)}), bf16[8,1024,128]{2,1,0:T(8,128)(2,1)S(1)}, u32[]{:S(2)}, u32[]{:S(2)}) async-start(bf16[8,1024,128]{2,1,0:T(8,128)(2,1)} %bitcast_bitcast_fusion), calls=%async_computation.1 | async-start | bytes 4194304 | tf_op jit(solution)/shard_map/all_to_all | solution.py:287
  50.6 4.6 %copy-start.2 = (bf16[8,1024,128]{2,1,0:T(8,128)(2,1)}, bf16[8,1024,128]{2,1,0:T(8,128)(2,1)S(1)}, u32[]{:S(2)}) copy-start(bf16[8,1024,128]{2,1,0:T(8,128)(2,1)S(1)} %all-to-all-done.1) | copy-start | bytes 6291460
  50.6 32.7 %all-to-all-start = ((bf16[8,1024,128]{2,1,0:T(8,128)(2,1)}), bf16[8,1024,128]{2,1,0:T(8,128)(2,1)}, u32[]{:S(2)}, u32[]{:S(2)}) async-start(bf16[8,1024,128]{2,1,0:T(8,128)(2,1)} %bitcast_bitcast_fusion.1), calls=%async_computation | async-start | bytes 4194304 | tf_op jit(solution)/shard_map/all_to_all | solution.py:287
  54.9 163.2 %reduce-scatter.2.cloned.1.call-start = ((), (), s32[]{:S(2)}) async-start(), calls=%async_computation.6 | async-start | bytes 4718592 | tf_op jit(solution)/shard_map/reduce_scatter | solution.py:297
  137.7 1.6 copy-start.4
  176.1 4.6 %copy-start.1 = (bf16[8192,128]{1,0:T(8,128)(2,1)S(1)}, bf16[8192,128]{1,0:T(8,128)(2,1)}, u32[]{:S(2)}) copy-start(bf16[8192,128]{1,0:T(8,128)(2,1)} %get-tuple-element.11) | copy-start | bytes 6291460
  176.1 42.1 %all-to-all-start.2 = ((bf16[8,1024,128]{2,1,0:T(8,128)(2,1)}), bf16[8,1024,128]{2,1,0:T(8,128)(2,1)}, u32[]{:S(2)}, u32[]{:S(2)}) async-start(bf16[8,1024,128]{2,1,0:T(8,128)(2,1)} %bitcast.53), calls=%async_computation.2 | async-start | bytes 4194304 | tf_op jit(solution)/shard_map/all_to_all | solution.py:305
  180.6 76.8 %all-reduce.2.cloned.1.call-start = ((), (), s32[]{:S(2)}) async-start(), calls=%async_computation.7 | async-start | bytes 1048576 | tf_op jit(solution)/shard_map/psum | solution.py:317
  183.8 34.4 %copy-start.3 = (bf16[1024,1024]{1,0:T(8,128)(2,1)S(1)}, bf16[1024,1024]{1,0:T(8,128)(2,1)}, u32[]{:S(2)}) copy-start(bf16[1024,1024]{1,0:T(8,128)(2,1)} %param.13) | copy-start | bytes 6291460
  183.8 34.4 %copy-start.5 = (f32[1024]{0:T(1024)S(1)}, f32[1024]{0:T(1024)}, u32[]{:S(2)}) copy-start(f32[1024]{0:T(1024)} %param.12) | copy-start | bytes 12292
Sparse Core Ops, SparseCore 0:
  9.9 54.7 all-gather.1
  137.9 68.6 reduce-scatter.1
  218.3 39.0 all-reduce.1
